TPU v7x, 128 devices: a whole 4x4x4 slice. The times are simulated.
128 devices in a mesh: section: 8 (over x_hi, y), rep: 16 (over x_lo, z, core).
Axes of the slice: x: 4 (x_hi: 2, x_lo: 2; x = x_hi * 2 + x_lo), y: 4, z: 4, core: 2. Of those that a mesh axis runs over, the one named last changes fastest.
Arguments:
- section_state: float32 [8, 4, 16, 196, 512], P('section', None, 'rep'), may hold values from -6 to 6
- arriving: float32 [2, 4, 16, 196, 512], P(None, None, 'rep'), may hold values from -6 to 6
- first_weight: float32 [8, 1, 9, 512, 128], P('section'), may hold values from -0.1875 to 0.1875
- second_weight: float32 [8, 1, 9, 512, 128], P('section'), may hold values from -0.1875 to 0.1875
Outputs:
- returned: float32 [8, 4, 16, 196, 512], P('section', None, 'rep')
- first_grad: float32 [8, 1, 9, 512, 128], P('section', None, None, 'rep')
- second_grad: float32 [8, 1, 9, 512, 128], P('section', None, None, 'rep')
All inputs are finite; a program needn't handle non-finite values.
Results may differ from a plain program's by a relative error of at most 0.00019.
Values sent between devices are 32-bit elements; how exact they have to be, the bound alone decides.
A program may use at most 128 MiB of HBM per device.

v0:
```python
import jax
import jax.numpy as jnp
from jax import lax
from jax.experimental import pallas as pl
from jax.experimental.pallas import tpu as pltpu
from jax.sharding import PartitionSpec as P

MESH = pl.DeviceIdType.MESH
F32, BF16 = jnp.float32, jnp.bfloat16
NT = (((1,), (1,)), ((), ()))
NN = (((1,), (0,)), ((), ()))
SIDE, PIX, PITCH, W, TAPS, GROUPS, TICKS, SECTIONS = 14, 196, 16, 128, 9, 4, 3, 8
ROWS = SIDE * PITCH
TOP = 24
FRAME = 304
HALF = 288
ORDERS = ((0, 1, 2), (1, 2, 0), (2, 0, 1))


def split(value):
    high = value.astype(BF16)
    return high, (value - high.astype(F32)).astype(BF16)


def expand(dense, frame):
    for row in range(SIDE):
        frame[pl.ds(TOP + PITCH * row, SIDE), :] = dense[pl.ds(SIDE * row, SIDE), :]


def compact(value, frame, dense):
    frame[pl.ds(TOP, ROWS), :] = value
    for row in range(SIDE):
        dense[pl.ds(SIDE * row, SIDE), :] = frame[pl.ds(TOP + PITCH * row, SIDE), :]


def shifted(frame, maps):
    for col in range(3):
        high, low = split(frame[pl.ds(TOP - PITCH - 1 + col, 256), :])
        maps[col, 0:256, :] = high
        maps[col, HALF : HALF + 256, :] = low


def tapped(maps):
    columns = []
    for tap in range(TAPS):
        row, col = divmod(tap, 3)
        first = PITCH * row
        columns.append(
            jnp.concatenate(
                [maps[col, first : first + ROWS, :], maps[col, HALF + first : HALF + first + ROWS, :]], axis=0
            )
        )
    return jnp.concatenate(columns, axis=1)


def conv(maps, weight, dims):
    out = lax.dot_general(tapped(maps), weight, dims, preferred_element_type=F32)
    return (out[:ROWS, :W] + out[:ROWS, W:]) + (out[ROWS:, :W] + out[ROWS:, W:])


def weight_grad(pulled, maps):
    high, low = split(pulled.T)
    columns = []
    for tap in range(TAPS):
        row, col = divmod(tap, 3)
        first = PITCH * row
        top = maps[col, first : first + 256, :]
        columns.append(jnp.concatenate([top, top, maps[col, HALF + first : HALF + first + 256, :]], axis=0))
    return lax.dot_general(
        jnp.concatenate([high, low, high], axis=1),
        jnp.concatenate(columns, axis=1),
        NN,
        preferred_element_type=F32,
    )


def kernel(
    state_ref, arriving_ref, first_ref, second_ref, ret_ref, fgrad_ref, sgrad_ref,
    raw, wfwd, wback, held, out, maps_y, maps_x, maps_p, der, into, e_two, frames, acc, pair, part1, part2, part3,
    wsem, lsem, ssem, rsem, osem, xsend, xrecv,
):
    section, rep = lax.axis_index("section"), lax.axis_index("rep")
    core, z, x = rep % 2, (rep // 2) % 4, rep // 8
    bit_b = z // 2
    bit_a = (z + bit_b) % 2
    bits = (x, bit_b, bit_a)

    def rep_of(x_, z_, core_):
        return x_ * 8 + z_ * 2 + core_

    across = (
        rep_of(1 - x, z, core),
        rep_of(x, 3 - z, core),
        rep_of(x, 2 * (z // 2) + 1 - z % 2, core),
    )
    mate = rep_of(x, z, 1 - core)
    below, above = (section + SECTIONS - 1) % SECTIONS, (section + 1) % SECTIONS

    barrier = pltpu.get_barrier_semaphore()
    for device in ((below, rep), (above, rep), (section, mate)) + tuple((section, r) for r in across):
        pl.semaphore_signal(barrier, inc=1, device_id=device, device_id_type=MESH)

    def lanes(g):
        return pl.ds(pl.multiple_of(g * W, W), W)

    def load_state(h, g):
        return pltpu.make_async_copy(state_ref.at[0, h, 0, :, lanes(g)], held.at[0, h, g], lsem.at[h, g])

    def load_weight(which, g):
        ref = (first_ref, second_ref)[which]
        return pltpu.make_async_copy(ref.at[0, 0, :, lanes(g), :], raw.at[which, g], wsem.at[which, g])

    def load_arriving(k, h, g):
        return pltpu.make_async_copy(
            arriving_ref.at[k, h, 0, :, lanes(g)], held.at[k + 1, h, g], rsem.at[k, h, g]
        )

    def send(k, h, g):
        return pltpu.make_async_remote_copy(
            src_ref=out.at[k, h, g],
            dst_ref=held.at[k + 1, h, g],
            send_sem=ssem.at[k, h, g],
            recv_sem=rsem.at[k, h, g],
            device_id=(below, rep),
            device_id_type=MESH,
        )

    def save(h, g):
        return pltpu.make_async_copy(out.at[2, h, g], ret_ref.at[0, h, 0, :, lanes(g)], osem.at[h, g])

    for g in range(GROUPS):
        load_state(0, g).start()
        load_weight(1, g).start()
        load_state(1, g).start()
        load_weight(0, g).start()
    for g in range(GROUPS):
        load_state(3, g).start()
        load_state(2, g).start()

    @pl.when(section == SECTIONS - 1)
    def _():
        for k in range(TICKS - 1):
            for h in range(4):
                for g in range(GROUPS):
                    load_arriving(k, h, g).start()

    frames[...] = jnp.zeros_like(frames)
    for maps in (maps_y, maps_x):
        maps[:, :, 256:HALF, :] = jnp.zeros((GROUPS, 3, HALF - 256, W), BF16)
        maps[:, :, HALF + 256 :, :] = jnp.zeros((GROUPS, 3, HALF - 256, W), BF16)
    maps_p[:, 256:HALF, :] = jnp.zeros((3, HALF - 256, W), BF16)
    maps_p[:, HALF + 256 :, :] = jnp.zeros((3, HALF - 256, W), BF16)
    inside = (lax.broadcasted_iota(jnp.int32, (ROWS, W), 0) & (PITCH - 1)) < SIDE
    frame_a, frame_b, frame_c, frame_d = (frames.at[i] for i in range(4))

    def arrive(k, h, g):
        if k == 0:
            load_state(h, g).wait()
            return

        @pl.when(section < SECTIONS - 1)
        def _():
            send(k - 1, h, g).wait_recv()

        @pl.when(section == SECTIONS - 1)
        def _():
            load_arriving(k - 1, h, g).wait()

    def leave(k, h, g):
        if k == TICKS - 1:
            save(h, g).start()
            return

        @pl.when(section > 0)
        def _():
            send(k, h, g).start()

    def prepare(which, g):
        load_weight(which, g).wait()
        for tap in range(TAPS):
            high, low = split(raw[which, g, tap])
            wfwd[which, g, 0:W, tap * W : (tap + 1) * W] = high
            wfwd[which, g, W : 2 * W, tap * W : (tap + 1) * W] = low
            back = (TAPS - 1 - tap) * W
            wback[which, g, back : back + W, 0:W] = high
            wback[which, g, back : back + W, W : 2 * W] = low

    def act_of(pre):
        gate = jax.nn.sigmoid(pre)
        return pre * gate, jnp.where(inside, gate * (1.0 + pre * (1.0 - gate)), 0.0)

    def collect(which, g, grad, fresh):
        for share in range(4):
            z_low, core_ = share // 2, share % 2
            place = acc.at[which, core_, g // 2, g % 2, (z_low + g % 2) % 2]
            rows = grad[32 * share : 32 * share + 32, :]
            place[...] = rows if fresh else place[...] + rows

    def rebuild(k, g):
        arrive(k, 0, g)
        if k == 0:
            prepare(1, g)
        expand(held.at[k, 0, g], frame_a)
        shifted(frame_a, maps_y.at[g])
        act, slope = act_of(conv(maps_y.at[g], wfwd[1, g], NT))
        der[1, g] = slope
        arrive(k, 1, g)
        expand(held.at[k, 1, g], frame_b)
        x_two = jnp.where(inside, frame_b[pl.ds(TOP, ROWS), :] - act, 0.0)
        compact(x_two, frame_c, out.at[k, 1, g])
        leave(k, 1, g)
        if k == 0:
            prepare(0, g)
        shifted(frame_c, maps_x.at[g])
        act, slope = act_of(conv(maps_x.at[g], wfwd[0, g], NT))
        der[0, g] = slope
        compact(frame_a[pl.ds(TOP, ROWS), :] - act, frame_d, out.at[k, 0, g])
        leave(k, 0, g)

    def pull_second(k, g):
        arrive(k, 3, g)
        expand(held.at[k, 3, g], frame_a)
        e_in = frame_a[pl.ds(TOP, ROWS), :]
        e_two[g] = e_in
        frame_c[pl.ds(TOP, ROWS), :] = e_in * der[1, g]
        shifted(frame_c, maps_p)
        into[g] = conv(maps_p, wback[1, g], NN)
        collect(1, g, weight_grad(frame_c[pl.ds(TOP, 256), :], maps_y.at[g]), k == 0)

    def pull_first(k, g):
        arrive(k, 2, g)
        expand(held.at[k, 2, g], frame_a)
        d_one = frame_a[pl.ds(TOP, ROWS), :] + into[g]
        compact(d_one, frame_d, out.at[k, 2, g])
        if k == TICKS - 1:
            leave(k, 2, g)
        frame_c[pl.ds(TOP, ROWS), :] = d_one * der[0, g]
        shifted(frame_c, maps_p)
        compact(e_two[g] + conv(maps_p, wback[0, g], NN), frame_d, out.at[k, 3, g])
        leave(k, 3, g)
        collect(0, g, weight_grad(frame_c[pl.ds(TOP, 256), :], maps_x.at[g]), k == 0)

    def each(function, k, first=0, last=GROUPS):
        def step(g, carry):
            function(k, g)
            return carry

        lax.fori_loop(first, last, step, 0)

    def exchange(which, level, third):
        cut = pl.ds(384 * third, 384)
        if level == 0:
            source, target, device = acc.at[which, 1 - core, :, :, :, :, cut], pair.at[which, :, :, :, :, cut], mate
        else:
            axis = ORDERS[third][level - 1]
            device = across[axis]
            if level == 1:
                index = [slice(None)] * 3
                index[axis] = 1 - bits[axis]
                source, target = pair.at[(which, *index, slice(None), cut)], part1.at[which, third]
            elif level == 2:
                rest = [a for a in range(3) if a != ORDERS[third][0]]
                index = [slice(None)] * 2
                index[rest.index(axis)] = 1 - bits[axis]
                source, target = part1.at[(which, third, *index)], part2.at[which, third]
            else:
                source, target = part2.at[which, third, 1 - bits[axis]], part3.at[which, third]
        return pltpu.make_async_remote_copy(
            src_ref=source,
            dst_ref=target,
            send_sem=xsend.at[which, level, third],
            recv_sem=xrecv.at[which, level, third],
            device_id=(section, device),
            device_id_type=MESH,
        )

    def absorb(which, level, third):
        exchange(which, level, third).wait_recv()
        cut = pl.ds(384 * third, 384)
        if level == 0:
            pair[which, :, :, :, :, cut] += acc[which, core, :, :, :, :, cut]
            return
        axis = ORDERS[third][level - 1]
        if level == 1:
            index = [slice(None)] * 3
            index[axis] = bits[axis]
            part1[which, third] += pair[(which, *index, slice(None), cut)]
        elif level == 2:
            rest = [a for a in range(3) if a != ORDERS[third][0]]
            index = [slice(None)] * 2
            index[rest.index(axis)] = bits[axis]
            part2[which, third] += part1[(which, third, *index)]
        else:
            total = part3[which, third] + part2[which, third, bits[axis]]
            grad_ref = (fgrad_ref, sgrad_ref)[which]
            for tap in range(3):
                grad_ref[0, 0, 3 * third + tap] = total[:, tap * W : (tap + 1) * W]

    def begin(which):
        for third in range(3):
            exchange(which, 0, third).start()

    def advance(which, level):
        for third in range(3):
            absorb(which, level, third)
            if level < 3:
                exchange(which, level + 1, third).start()

    pl.semaphore_wait(barrier, 6)
    for k in range(TICKS - 1):
        each(rebuild, k)
        each(pull_second, k)
        each(pull_first, k)
        each(lambda k, g: leave(k, 2, g), k)
    last = TICKS - 1
    each(rebuild, last)
    each(pull_second, last)
    begin(1)
    each(pull_first, last, 0, 2)
    advance(1, 0)
    each(pull_first, last, 2, 4)
    begin(0)
    advance(1, 1)
    advance(0, 0)
    advance(1, 2)
    advance(0, 1)
    advance(1, 3)
    advance(0, 2)
    advance(0, 3)

    def drain(g, carry):
        for h in range(4):
            save(h, g).wait()
        return carry

    lax.fori_loop(0, GROUPS, drain, 0)

    @pl.when(section > 0)
    def _():
        def drain_sent(g, carry):
            for k in range(TICKS - 1):
                for h in range(4):
                    send(k, h, g).wait_send()
            return carry

        lax.fori_loop(0, GROUPS, drain_sent, 0)

    for which in range(2):
        for level in range(4):
            for third in range(3):
                exchange(which, level, third).wait_send()


def on_device(section_state, arriving, first_weight, second_weight):
    anywhere = pl.BlockSpec(memory_space=pl.ANY)
    vmem = pl.BlockSpec(memory_space=pltpu.VMEM)
    dma = pltpu.SemaphoreType.DMA
    share = jax.ShapeDtypeStruct((1, 1, TAPS, 32, W), F32)
    return pl.pallas_call(
        kernel,
        out_shape=(jax.ShapeDtypeStruct(section_state.shape, F32), share, share),
        in_specs=[anywhere] * 4,
        out_specs=(anywhere, vmem, vmem),
        scratch_shapes=[
            pltpu.VMEM((2, GROUPS, TAPS, W, W), F32),
            pltpu.VMEM((2, GROUPS, 2 * W, TAPS * W), BF16),
            pltpu.VMEM((2, GROUPS, TAPS * W, 2 * W), BF16),
            pltpu.VMEM((TICKS, 4, GROUPS, PIX, W), F32),
            pltpu.VMEM((TICKS, 4, GROUPS, PIX, W), F32),
            pltpu.VMEM((GROUPS, 3, 2 * HALF, W), BF16),
            pltpu.VMEM((GROUPS, 3, 2 * HALF, W), BF16),
            pltpu.VMEM((3, 2 * HALF, W), BF16),
            pltpu.VMEM((2, GROUPS, ROWS, W), F32),
            pltpu.VMEM((GROUPS, ROWS, W), F32),
            pltpu.VMEM((GROUPS, ROWS, W), F32),
            pltpu.VMEM((4, FRAME, W), F32),
            pltpu.VMEM((2, 2, 2, 2, 2, 32, TAPS * W), F32),
            pltpu.VMEM((2, 2, 2, 2, 32, TAPS * W), F32),
            pltpu.VMEM((2, 3, 2, 2, 32, 384), F32),
            pltpu.VMEM((2, 3, 2, 32, 384), F32),
            pltpu.VMEM((2, 3, 32, 384), F32),
            dma((2, GROUPS)),
            dma((4, GROUPS)),
            dma((TICKS - 1, 4, GROUPS)),
            dma((TICKS - 1, 4, GROUPS)),
            dma((4, GROUPS)),
            dma((2, 4, 3)),
            dma((2, 4, 3)),
        ],
        compiler_params=pltpu.CompilerParams(
            collective_id=0, has_side_effects=True, vmem_limit_bytes=60 * 2**20
        ),
        name="relay",
    )(section_state, arriving, first_weight, second_weight)


def solution(mesh):
    return jax.shard_map(
        on_device,
        mesh=mesh,
        in_specs=(
            P("section", None, "rep", None, None),
            P(None, None, "rep", None, None),
            P("section", None, None, None, None),
            P("section", None, None, None, None),
        ),
        out_specs=(
            P("section", None, "rep", None, None),
            P("section", None, None, "rep", None),
            P("section", None, None, "rep", None),
        ),
        check_vma=False,
    )
```

profile of v0, /device:TPU:6, one launch (start us, length us, event | category | flops | bytes accessed | tf_op | source)
XLA Modules:
  0.0 110.7 jit_solution(2662491011183533568)
XLA Ops:
  0.6 0.0 copy-start
  0.6 2.9 %copy.7.state_ref = f32[1,4,1,196,512]{4,3,2,1,0:T(8,128)} copy(f32[1,4,1,196,512]{4,2,3,1,0:T(1,128)} %param.4) | data formatting | bytes 3211264 | tf_op args[0]
  3.5 0.0 copy-done
  3.5 2.1 %copy.8.arriving_ref = f32[2,4,1,196,512]{4,3,2,1,0:T(8,128)} copy(f32[2,4,1,196,512]{4,2,3,1,0:T(1,128)S(1)} %copy-done) | data formatting | bytes 6422528 | tf_op args[1]
  5.7 99.4 %relay.1 = (f32[1,4,1,196,512]{4,3,2,1,0:T(8,128)}, f32[1,1,9,32,128]{4,3,2,1,0:T(8,128)}, f32[1,1,9,32,128]{4,3,2,1,0:T(8,128)}) custom-call(f32[1,4,1,196,512]{4,3,2,1,0:T(8,128)} %copy.7.state_ref, f32[2,4,1,196,512]{4,3,2,1,0:T(8,128)} %copy.8.arriving_ref, f32[1,1,9,512,128]{4,3,2,1,0:T(8,128)} %first_ref.1, f32[1,1,9,512,128]{4,3,2,1,0:T(8,128)} %second_ref.1), custom_call_target="tpu_custom_call" | custom-call | tf_op jit(solution)/shard_map/relay/pallas_call | solution.py:359
  105.1 0.0 copy-start.2
  105.1 0.0 copy-start.1
  105.1 4.3 %copy.9 = f32[1,4,1,196,512]{4,2,3,1,0:T(1,128)} copy(f32[1,4,1,196,512]{4,3,2,1,0:T(8,128)} %get-tuple-element.3) | data formatting | bytes 3211264 | tf_op jit(solution)/shard_map/relay/pallas_call | solution.py:359
  109.4 0.0 copy-done.2
  109.4 0.7 copy.12
  110.0 0.0 copy-done.1
  110.0 0.7 copy.13
Async XLA Ops:
  0.6 2.9 %copy-start = (f32[2,4,1,196,512]{4,2,3,1,0:T(1,128)S(1)}, f32[2,4,1,196,512]{4,2,3,1,0:T(1,128)}, u32[]{:S(2)}) copy-start(f32[2,4,1,196,512]{4,2,3,1,0:T(1,128)} %param.5) | copy-start | bytes 9633796
  105.1 4.3 %copy-start.2 = (f32[1,1,9,32,128]{4,3,2,1,0:T(8,128)S(1)}, f32[1,1,9,32,128]{4,3,2,1,0:T(8,128)}, u32[]{:S(2)}) copy-start(f32[1,1,9,32,128]{4,3,2,1,0:T(8,128)} %get-tuple-element.10) | copy-start | bytes 442372
  105.1 5.0 %copy-start.1 = (f32[1,1,9,32,128]{4,3,2,1,0:T(8,128)S(1)}, f32[1,1,9,32,128]{4,3,2,1,0:T(8,128)}, u32[]{:S(2)}) copy-start(f32[1,1,9,32,128]{4,3,2,1,0:T(8,128)} %get-tuple-element.11) | copy-start | bytes 442372
where the time goes:
time: 112 us; the launch traced here: 111 us
  Pallas kernels  99.4 us (89%)
  local copies, waits for them, and re-layouts  10.7 us (10%)
    pallas_call x1, Pallas kernels, on_device(): pl.pallas_call(kernel, out_shape=(jax.ShapeDtypeStruct(section_state.shap...  99.4 us
    unnamed x10, local copies, waits for them, and re-layouts  6.38 us
    pallas_call x1, local copies, waits for them, and re-layouts, on_device(): pl.pallas_call(kernel, out_shape=(jax.ShapeDtypeStruct(section_state.shap...  4.28 us

commit v1 on v0

--- a/solution.py
+++ b/solution.py
@@ -76,8 +76,8 @@
 
 def kernel(
     state_ref, arriving_ref, first_ref, second_ref, ret_ref, fgrad_ref, sgrad_ref,
-    raw, wfwd, wback, held, out, maps_y, maps_x, maps_p, der, into, e_two, frames, acc, pair, part1, part2, part3,
-    wsem, lsem, ssem, rsem, osem, xsend, xrecv,
+    raw, wfwd, wback, held, out, stop, maps_y, maps_x, maps_p, der, into, e_two, frames, acc, pair, part1, part2, part3,
+    wsem, lsem, ssem, rsem, osem, xsend, xrecv, psend, precv, hop_send, hop_recv,
 ):
     section, rep = lax.axis_index("section"), lax.axis_index("rep")
     core, z, x = rep % 2, (rep // 2) % 4, rep // 8
@@ -96,15 +96,24 @@
     mate = rep_of(x, z, 1 - core)
     below, above = (section + SECTIONS - 1) % SECTIONS, (section + 1) % SECTIONS
 
+    def around(steps):
+        return (section // 4) * 4 + (section + steps) % 4
+
+    came = (around(3), around(2))
+
+    shortcut = (9 - section) % SECTIONS
+
     barrier = pltpu.get_barrier_semaphore()
-    for device in ((below, rep), (above, rep), (section, mate)) + tuple((section, r) for r in across):
+    for device in ((below, rep), (above, rep), (around(1), rep), (around(3), rep), (shortcut, rep), (section, mate)) + tuple(
+        (section, r) for r in across
+    ):
         pl.semaphore_signal(barrier, inc=1, device_id=device, device_id_type=MESH)
 
     def lanes(g):
         return pl.ds(pl.multiple_of(g * W, W), W)
 
     def load_state(h, g):
-        return pltpu.make_async_copy(state_ref.at[0, h, 0, :, lanes(g)], held.at[0, h, g], lsem.at[h, g])
+        return pltpu.make_async_copy(state_ref.at[h, :, 0, lanes(g)], held.at[0, h, g], lsem.at[h, g])
 
     def load_weight(which, g):
         ref = (first_ref, second_ref)[which]
@@ -112,7 +121,7 @@
 
     def load_arriving(k, h, g):
         return pltpu.make_async_copy(
-            arriving_ref.at[k, h, 0, :, lanes(g)], held.at[k + 1, h, g], rsem.at[k, h, g]
+            arriving_ref.at[k, h, :, 0, lanes(g)], held.at[k + 1, h, g], rsem.at[k, h, g]
         )
 
     def send(k, h, g):
@@ -125,8 +134,29 @@
             device_id_type=MESH,
         )
 
+    def relayed(k, h, hop):
+        source = (out.at[k, h, 0], stop.at[0, k, h], stop.at[1, k, h])[hop]
+        target = (stop.at[0, k, h], stop.at[1, k, h], held.at[k + 1, h, 0])[hop]
+        device = (around(1), around(1), (came[1] + SECTIONS - 1) % SECTIONS)[hop]
+        arrived = rsem.at[k, h, 0] if hop == 2 else hop_recv.at[hop, k, h]
+        return pltpu.make_async_remote_copy(
+            src_ref=source,
+            dst_ref=target,
+            send_sem=hop_send.at[hop, k, h],
+            recv_sem=arrived,
+            device_id=(device, rep),
+            device_id_type=MESH,
+        )
+
+    def pass_on(k, hop, halves):
+        @pl.when(came[hop - 1] > 0)
+        def _():
+            for h in halves:
+                relayed(k, h, hop - 1).wait_recv()
+                relayed(k, h, hop).start()
+
     def save(h, g):
-        return pltpu.make_async_copy(out.at[2, h, g], ret_ref.at[0, h, 0, :, lanes(g)], osem.at[h, g])
+        return pltpu.make_async_copy(out.at[2, h, g], ret_ref.at[h, :, 0, lanes(g)], osem.at[h, g])
 
     for g in range(GROUPS):
         load_state(0, g).start()
@@ -171,9 +201,13 @@
             save(h, g).start()
             return
 
-        @pl.when(section > 0)
+        @pl.when((section > 0) & (g > 0))
         def _():
             send(k, h, g).start()
+
+        @pl.when((section > 0) & (g == 0))
+        def _():
+            relayed(k, h, 0).start()
 
     def prepare(which, g):
         load_weight(which, g).wait()
@@ -234,15 +268,21 @@
         compact(d_one, frame_d, out.at[k, 2, g])
         if k == TICKS - 1:
             leave(k, 2, g)
+        else:
+
+            @pl.when((section > 0) & (g == 0))
+            def _():
+                relayed(k, 2, 0).start()
+
         frame_c[pl.ds(TOP, ROWS), :] = d_one * der[0, g]
         shifted(frame_c, maps_p)
         compact(e_two[g] + conv(maps_p, wback[0, g], NN), frame_d, out.at[k, 3, g])
         leave(k, 3, g)
         collect(0, g, weight_grad(frame_c[pl.ds(TOP, 256), :], maps_x.at[g]), k == 0)
 
-    def each(function, k, first=0, last=GROUPS):
-        def step(g, carry):
-            function(k, g)
+    def each(function, k, first=0, last=GROUPS, turn=0):
+        def step(i, carry):
+            function(k, (i + turn) % GROUPS if turn else i)
             return carry
 
         lax.fori_loop(first, last, step, 0)
@@ -250,7 +290,16 @@
     def exchange(which, level, third):
         cut = pl.ds(384 * third, 384)
         if level == 0:
-            source, target, device = acc.at[which, 1 - core, :, :, :, :, cut], pair.at[which, :, :, :, :, cut], mate
+            g = third
+            source, target = acc.at[which, 1 - core, g // 2, g % 2], pair.at[which, g // 2, g % 2]
+            return pltpu.make_async_remote_copy(
+                src_ref=source,
+                dst_ref=target,
+                send_sem=psend.at[which, g],
+                recv_sem=precv.at[which, g],
+                device_id=(section, mate),
+                device_id_type=MESH,
+            )
         else:
             axis = ORDERS[third][level - 1]
             device = across[axis]
@@ -278,7 +327,7 @@
         exchange(which, level, third).wait_recv()
         cut = pl.ds(384 * third, 384)
         if level == 0:
-            pair[which, :, :, :, :, cut] += acc[which, core, :, :, :, :, cut]
+            pair[which, third // 2, third % 2] += acc[which, core, third // 2, third % 2]
             return
         axis = ORDERS[third][level - 1]
         if level == 1:
@@ -296,31 +345,63 @@
             for tap in range(3):
                 grad_ref[0, 0, 3 * third + tap] = total[:, tap * W : (tap + 1) * W]
 
-    def begin(which):
-        for third in range(3):
-            exchange(which, 0, third).start()
-
     def advance(which, level):
         for third in range(3):
-            absorb(which, level, third)
+            if level > 0:
+                absorb(which, level, third)
             if level < 3:
                 exchange(which, level + 1, third).start()
 
-    pl.semaphore_wait(barrier, 6)
-    for k in range(TICKS - 1):
-        each(rebuild, k)
-        each(pull_second, k)
-        each(pull_first, k)
-        each(lambda k, g: leave(k, 2, g), k)
+    pl.semaphore_wait(barrier, 9)
+    xs, ds = (1, 0), (3, 2)
+
+    def rebuild_1(k, g):
+        rebuild(k, g)
+
+        @pl.when(g == 1)
+        def _():
+            pass_on(k - 1, 2, ds)
+
+    each(rebuild, 0)
+    pass_on(0, 1, xs)
+    each(pull_second, 0)
+    pass_on(0, 2, xs)
+    each(pull_first, 0)
+    pass_on(0, 1, ds)
+    each(lambda k, g: leave(k, 2, g), 0, 1)
+    each(rebuild_1, 1)
+    pass_on(1, 1, xs)
+    each(pull_second, 1, turn=1)
+    pass_on(1, 2, xs)
+    each(pull_first, 1)
+    pass_on(1, 1, ds)
+    each(lambda k, g: leave(k, 2, g), 1, 1)
     last = TICKS - 1
-    each(rebuild, last)
-    each(pull_second, last)
-    begin(1)
-    each(pull_first, last, 0, 2)
+    each(rebuild_1, last)
+
+    def last_second(k, g):
+        pull_second(k, g)
+        exchange(1, 0, g).start()
+
+        @pl.when(g > 0)
+        def _():
+            absorb(1, 0, g - 1)
+
+    def last_first(k, g):
+        pull_first(k, g)
+        exchange(0, 0, g).start()
+
+        @pl.when(g > 0)
+        def _():
+            absorb(0, 0, g - 1)
+
+    each(last_second, last)
+    absorb(1, 0, 3)
     advance(1, 0)
-    each(pull_first, last, 2, 4)
-    begin(0)
+    each(last_first, last, 0, 2)
     advance(1, 1)
+    each(last_first, last, 2, 4)
+    absorb(0, 0, 3)
     advance(0, 0)
     advance(1, 2)
     advance(0, 1)
@@ -343,12 +424,35 @@
                     send(k, h, g).wait_send()
             return carry
 
-        lax.fori_loop(0, GROUPS, drain_sent, 0)
+        lax.fori_loop(1, GROUPS, drain_sent, 0)
+
+    for hop, condition in enumerate((section > 0, came[0] > 0, came[1] > 0)):
+
+        @pl.when(condition)
+        def _(hop=hop):
+            for k in range(TICKS - 1):
+                for h in range(4):
+                    relayed(k, h, hop).wait_send()
 
     for which in range(2):
         for level in range(4):
-            for third in range(3):
+            for third in range(3 if level else GROUPS):
                 exchange(which, level, third).wait_send()
+
+
+def hand_out(*refs):
+    sources, results, (buffer, grads, insem, outsem) = refs[:3], refs[3:6], refs[6:]
+    pieces = [(sources[0].at[h], buffer.at[h], results[0].at[h]) for h in range(4)]
+    pieces += [(sources[i].at[0, 0], grads.at[i - 1], results[i].at[0, 0]) for i in (1, 2)]
+    fetches = [pltpu.make_async_copy(a, b, insem.at[i]) for i, (a, b, _) in enumerate(pieces)]
+    stores = [pltpu.make_async_copy(b, c, outsem.at[i]) for i, (_, b, c) in enumerate(pieces)]
+    for fetch in fetches:
+        fetch.start()
+    for fetch, store in zip(fetches, stores):
+        fetch.wait()
+        store.start()
+    for store in stores:
+        store.wait()
 
 
 def on_device(section_state, arriving, first_weight, second_weight):
@@ -356,9 +460,11 @@
     vmem = pl.BlockSpec(memory_space=pltpu.VMEM)
     dma = pltpu.SemaphoreType.DMA
     share = jax.ShapeDtypeStruct((1, 1, TAPS, 32, W), F32)
-    return pl.pallas_call(
+    state = section_state.reshape(4, PIX, 1, GROUPS * W)
+    coming = arriving.reshape(TICKS - 1, 4, PIX, 1, GROUPS * W)
+    results = pl.pallas_call(
         kernel,
-        out_shape=(jax.ShapeDtypeStruct(section_state.shape, F32), share, share),
+        out_shape=(jax.ShapeDtypeStruct(state.shape, F32), share, share),
         in_specs=[anywhere] * 4,
         out_specs=(anywhere, vmem, vmem),
         scratch_shapes=[
@@ -367,6 +473,7 @@
             pltpu.VMEM((2, GROUPS, TAPS * W, 2 * W), BF16),
             pltpu.VMEM((TICKS, 4, GROUPS, PIX, W), F32),
             pltpu.VMEM((TICKS, 4, GROUPS, PIX, W), F32),
+            pltpu.VMEM((2, TICKS - 1, 4, PIX, W), F32),
             pltpu.VMEM((GROUPS, 3, 2 * HALF, W), BF16),
             pltpu.VMEM((GROUPS, 3, 2 * HALF, W), BF16),
             pltpu.VMEM((3, 2 * HALF, W), BF16),
@@ -386,12 +493,25 @@
             dma((4, GROUPS)),
             dma((2, 4, 3)),
             dma((2, 4, 3)),
+            dma((2, GROUPS)),
+            dma((2, GROUPS)),
+            dma((3, TICKS - 1, 4)),
+            dma((2, TICKS - 1, 4)),
         ],
         compiler_params=pltpu.CompilerParams(
             collective_id=0, has_side_effects=True, vmem_limit_bytes=60 * 2**20
         ),
         name="relay",
-    )(section_state, arriving, first_weight, second_weight)
+    )(state, coming, first_weight, second_weight)
+    returned, first_grad, second_grad = pl.pallas_call(
+        hand_out,
+        out_shape=(jax.ShapeDtypeStruct(state.shape, F32), share, share),
+        in_specs=[anywhere] * 3,
+        out_specs=(anywhere,) * 3,
+        scratch_shapes=[pltpu.VMEM(state.shape, F32), pltpu.VMEM((2, TAPS, 32, W), F32), dma((6,)), dma((6,))],
+        name="hand_out",
+    )(*results)
+    return returned.reshape(section_state.shape), first_grad, second_grad
 
 
 def solution(mesh):

time: 112 us -> 103 us (0.920)
  the two profiles are of different devices: /device:TPU:6 before, /device:TPU:8 now
where the time goes in v1:
time: 103 us
  Pallas kernels  102 us (99%)
    pallas_call x1, Pallas kernels, on_device(): pl.pallas_call(kernel, out_shape=(jax.ShapeDtypeStruct(state.shape, F32),...  99.9 us
    pallas_call x1, Pallas kernels, on_device(): pl.pallas_call(hand_out, out_shape=(jax.ShapeDtypeStruct(state.shape, F32...  2.34 us

profile of v1, /device:TPU:8, one launch (start us, length us, event | category | flops | bytes accessed | tf_op | source)
XLA Modules:
  0.0 102.9 jit_solution(4702203450811427794)
XLA Ops:
  0.6 99.9 %relay.1 = (f32[4,196,1,512]{3,2,1,0:T(1,128)}, f32[1,1,9,32,128]{4,3,2,1,0:T(8,128)}, f32[1,1,9,32,128]{4,3,2,1,0:T(8,128)}) custom-call(f32[4,196,1,512]{3,2,1,0:T(1,128)} %bitcast.6, f32[2,4,196,1,512]{4,3,2,1,0:T(1,128)} %bitcast.5, f32[1,1,9,512,128]{4,3,2,1,0:T(8,128)} %first_ref.1, f32[1,1,9,512,128]{4,3,2,1,0:T(8,128)} %second_ref.1), custom_call_target="tpu_custom_call" | custom-call | tf_op jit(solution)/shard_map/relay/pallas_call | solution.py:465
  100.6 2.3 %hand_out.1 = (f32[4,196,1,512]{3,2,1,0:T(1,128)}, f32[1,1,9,32,128]{4,3,2,1,0:T(8,128)}, f32[1,1,9,32,128]{4,3,2,1,0:T(8,128)}) custom-call(f32[4,196,1,512]{3,2,1,0:T(1,128)} %get-tuple-element.9.refs_0_, f32[1,1,9,32,128]{4,3,2,1,0:T(8,128)} %get-tuple-element.10.refs_1_, f32[1,1,9,32,128]{4,3,2,1,0:T(8,128)} %get-tuple-element.11.refs_2_), custom_call_target="tpu_custom_call" | custom-call | tf_op jit(solution)/shard_map/hand_out/pallas_call | solution.py:506

commit v2 on v1

--- a/solution.py
+++ b/solution.py
@@ -16,6 +16,23 @@
 HALF = 288
 ORDERS = ((0, 1, 2), (1, 2, 0), (2, 0, 1))
 
+ROUND = (
+    ((0, 1), (1, 0), (2, 0)),
+    ((0, 2), (0, 3), (1, 3)),
+)
+STOPS = 3
+PLAN = (
+    ("R", 0, 0, (), (("h1", 0, 1, 0),)),
+    ("P2", 0, 0, (("h1", 0, 0, 1),), (("h2", 0, 1, 0),)),
+    ("P1", 0, 0, (("S", 0, 3, 0), ("S", 0, 3, 1), ("S", 0, 2, 1), ("h2", 0, 0, 1)), (("S", 0, 2, 0), ("h1", 0, 2, 0), ("S", 0, 3, 3), ("S", 0, 2, 3), ("S", 0, 3, 2))),
+    ("R", 1, 1, (("S", 0, 2, 2), ("h1", 1, 1, 3)), ()),
+    ("P2", 1, 0, (("h1", 1, 0, 2),), (("h1", 1, 0, 3), ("h2", 0, 2, 0))),
+    ("P1", 1, 1, (("S", 1, 3, 3), ("S", 1, 3, 2), ("h2", 1, 0, 2), ("h2", 1, 1, 3)), (("S", 1, 3, 0), ("S", 1, 3, 1), ("h2", 1, 0, 3), ("S", 1, 2, 1))),
+    ("R", 2, 0, (), (("S", 1, 2, 0), ("S", 1, 2, 2), ("S", 1, 2, 3))),
+    ("P2", 2, 0, (), ()),
+    ("P1", 2, 0, (("rs", 1, 0),), (("rs", 0, 0), ("rs", 1, 1), ("rs", 0, 1), ("rs", 1, 2), ("rs", 0, 2), ("rs", 1, 3), ("rs", 0, 3))),
+)
+
 
 def split(value):
     high = value.astype(BF16)
@@ -40,22 +57,22 @@
         maps[col, HALF : HALF + 256, :] = low
 
 
-def tapped(maps):
-    columns = []
-    for tap in range(TAPS):
-        row, col = divmod(tap, 3)
-        first = PITCH * row
-        columns.append(
-            jnp.concatenate(
-                [maps[col, first : first + ROWS, :], maps[col, HALF + first : HALF + first + ROWS, :]], axis=0
-            )
-        )
-    return jnp.concatenate(columns, axis=1)
-
-
-def conv(maps, weight, dims):
-    out = lax.dot_general(tapped(maps), weight, dims, preferred_element_type=F32)
+def tap_of(maps, tap):
+    row, col = divmod(tap, 3)
+    first = PITCH * row
+    return maps[col, first : first + ROWS, :], maps[col, HALF + first : HALF + first + ROWS, :]
+
+
+def conv(maps, weight):
+    columns = [jnp.concatenate(tap_of(maps, tap), axis=0) for tap in range(TAPS)]
+    out = lax.dot_general(jnp.concatenate(columns, axis=1), weight, NT, preferred_element_type=F32)
     return (out[:ROWS, :W] + out[:ROWS, W:]) + (out[ROWS:, :W] + out[ROWS:, W:])
+
+
+def conv_back(maps, weight):
+    columns = [piece for tap in range(TAPS) for piece in tap_of(maps, tap)]
+    out = lax.dot_general(jnp.concatenate(columns, axis=1), weight, NN, preferred_element_type=F32)
+    return out[:, :W] + out[:, W:]
 
 
 def weight_grad(pulled, maps):
@@ -134,26 +151,26 @@
             device_id_type=MESH,
         )
 
-    def relayed(k, h, hop):
-        source = (out.at[k, h, 0], stop.at[0, k, h], stop.at[1, k, h])[hop]
-        target = (stop.at[0, k, h], stop.at[1, k, h], held.at[k + 1, h, 0])[hop]
+    def relayed(k, h, g, hop):
+        i = ROUND[k].index((h, g))
+        source = (out.at[k, h, g], stop.at[0, k, i], stop.at[1, k, i])[hop]
+        target = (stop.at[0, k, i], stop.at[1, k, i], held.at[k + 1, h, g])[hop]
         device = (around(1), around(1), (came[1] + SECTIONS - 1) % SECTIONS)[hop]
-        arrived = rsem.at[k, h, 0] if hop == 2 else hop_recv.at[hop, k, h]
+        arrived = rsem.at[k, h, g] if hop == 2 else hop_recv.at[hop, k, i]
         return pltpu.make_async_remote_copy(
             src_ref=source,
             dst_ref=target,
-            send_sem=hop_send.at[hop, k, h],
+            send_sem=hop_send.at[hop, k, i],
             recv_sem=arrived,
             device_id=(device, rep),
             device_id_type=MESH,
         )
 
-    def pass_on(k, hop, halves):
+    def pass_on(k, h, g, hop):
         @pl.when(came[hop - 1] > 0)
         def _():
-            for h in halves:
-                relayed(k, h, hop - 1).wait_recv()
-                relayed(k, h, hop).start()
+            relayed(k, h, g, hop - 1).wait_recv()
+            relayed(k, h, g, hop).start()
 
     def save(h, g):
         return pltpu.make_async_copy(out.at[2, h, g], ret_ref.at[h, :, 0, lanes(g)], osem.at[h, g])
@@ -178,10 +195,10 @@
     for maps in (maps_y, maps_x):
         maps[:, :, 256:HALF, :] = jnp.zeros((GROUPS, 3, HALF - 256, W), BF16)
         maps[:, :, HALF + 256 :, :] = jnp.zeros((GROUPS, 3, HALF - 256, W), BF16)
-    maps_p[:, 256:HALF, :] = jnp.zeros((3, HALF - 256, W), BF16)
-    maps_p[:, HALF + 256 :, :] = jnp.zeros((3, HALF - 256, W), BF16)
+    maps_p[:, :, 256:HALF, :] = jnp.zeros((2, 3, HALF - 256, W), BF16)
+    maps_p[:, :, HALF + 256 :, :] = jnp.zeros((2, 3, HALF - 256, W), BF16)
     inside = (lax.broadcasted_iota(jnp.int32, (ROWS, W), 0) & (PITCH - 1)) < SIDE
-    frame_a, frame_b, frame_c, frame_d = (frames.at[i] for i in range(4))
+    frame_a, frame_b, frame_c, frame_d = ([frames.at[i, j] for j in range(2)] for i in range(4))
 
     def arrive(k, h, g):
         if k == 0:
@@ -201,13 +218,17 @@
             save(h, g).start()
             return
 
-        @pl.when((section > 0) & (g > 0))
+        direct = section > 0
+        for group in [g_ for h_, g_ in ROUND[k] if h_ == h]:
+            direct = direct & (g != group)
+
+            @pl.when((section > 0) & (g == group))
+            def _(group=group):
+                relayed(k, h, group, 0).start()
+
+        @pl.when(direct)
         def _():
             send(k, h, g).start()
-
-        @pl.when((section > 0) & (g == 0))
-        def _():
-            relayed(k, h, 0).start()
 
     def prepare(which, g):
         load_weight(which, g).wait()
@@ -215,9 +236,11 @@
             high, low = split(raw[which, g, tap])
             wfwd[which, g, 0:W, tap * W : (tap + 1) * W] = high
             wfwd[which, g, W : 2 * W, tap * W : (tap + 1) * W] = low
-            back = (TAPS - 1 - tap) * W
+            back = (TAPS - 1 - tap) * 2 * W
             wback[which, g, back : back + W, 0:W] = high
             wback[which, g, back : back + W, W : 2 * W] = low
+            wback[which, g, back + W : back + 2 * W, 0:W] = high
+            wback[which, g, back + W : back + 2 * W, W : 2 * W] = jnp.zeros((W, W), BF16)
 
     def act_of(pre):
         gate = jax.nn.sigmoid(pre)
@@ -230,62 +253,79 @@
             rows = grad[32 * share : 32 * share + 32, :]
             place[...] = rows if fresh else place[...] + rows
 
-    def rebuild(k, g):
-        arrive(k, 0, g)
-        if k == 0:
-            prepare(1, g)
-        expand(held.at[k, 0, g], frame_a)
-        shifted(frame_a, maps_y.at[g])
-        act, slope = act_of(conv(maps_y.at[g], wfwd[1, g], NT))
-        der[1, g] = slope
-        arrive(k, 1, g)
-        expand(held.at[k, 1, g], frame_b)
-        x_two = jnp.where(inside, frame_b[pl.ds(TOP, ROWS), :] - act, 0.0)
-        compact(x_two, frame_c, out.at[k, 1, g])
-        leave(k, 1, g)
-        if k == 0:
-            prepare(0, g)
-        shifted(frame_c, maps_x.at[g])
-        act, slope = act_of(conv(maps_x.at[g], wfwd[0, g], NT))
-        der[0, g] = slope
-        compact(frame_a[pl.ds(TOP, ROWS), :] - act, frame_d, out.at[k, 0, g])
-        leave(k, 0, g)
-
-    def pull_second(k, g):
-        arrive(k, 3, g)
-        expand(held.at[k, 3, g], frame_a)
-        e_in = frame_a[pl.ds(TOP, ROWS), :]
-        e_two[g] = e_in
-        frame_c[pl.ds(TOP, ROWS), :] = e_in * der[1, g]
-        shifted(frame_c, maps_p)
-        into[g] = conv(maps_p, wback[1, g], NN)
-        collect(1, g, weight_grad(frame_c[pl.ds(TOP, 256), :], maps_y.at[g]), k == 0)
-
-    def pull_first(k, g):
-        arrive(k, 2, g)
-        expand(held.at[k, 2, g], frame_a)
-        d_one = frame_a[pl.ds(TOP, ROWS), :] + into[g]
-        compact(d_one, frame_d, out.at[k, 2, g])
+    def rebuild(k, pair_):
+        both = [(j, 2 * pair_ + j) for j in range(2)]
+        for _, g in both:
+            arrive(k, 1, g)
+            arrive(k, 0, g)
+            if k == 0:
+                prepare(1, g)
+        for j, g in both:
+            expand(held.at[k, 0, g], frame_a[j])
+            expand(held.at[k, 1, g], frame_b[j])
+        for j, g in both:
+            shifted(frame_a[j], maps_y.at[g])
+        acts = [act_of(conv(maps_y.at[g], wfwd[1, g])) for _, g in both]
+        for (j, g), (act, slope) in zip(both, acts):
+            der[1, g] = slope
+            compact(jnp.where(inside, frame_b[j][pl.ds(TOP, ROWS), :] - act, 0.0), frame_c[j], out.at[k, 1, g])
+        for _, g in both:
+            leave(k, 1, g)
+            if k == 0:
+                prepare(0, g)
+        for j, g in both:
+            shifted(frame_c[j], maps_x.at[g])
+        acts = [act_of(conv(maps_x.at[g], wfwd[0, g])) for _, g in both]
+        for (j, g), (act, slope) in zip(both, acts):
+            der[0, g] = slope
+            compact(frame_a[j][pl.ds(TOP, ROWS), :] - act, frame_d[j], out.at[k, 0, g])
+        for _, g in both:
+            leave(k, 0, g)
+
+    def pull_second(k, pair_):
+        both = [(j, 2 * pair_ + j) for j in range(2)]
+        for _, g in both:
+            arrive(k, 3, g)
+        for j, g in both:
+            expand(held.at[k, 3, g], frame_a[j])
+        for j, g in both:
+            e_in = frame_a[j][pl.ds(TOP, ROWS), :]
+            e_two[g] = e_in
+            frame_c[j][pl.ds(TOP, ROWS), :] = e_in * der[1, g]
+        for j, _ in both:
+            shifted(frame_c[j], maps_p.at[j])
+        pulled = [conv_back(maps_p.at[j], wback[1, g]) for j, g in both]
+        grads = [weight_grad(frame_c[j][pl.ds(TOP, 256), :], maps_y.at[g]) for j, g in both]
+        for (_, g), value, grad in zip(both, pulled, grads):
+            into[g] = value
+            collect(1, g, grad, k == 0)
         if k == TICKS - 1:
-            leave(k, 2, g)
-        else:
-
-            @pl.when((section > 0) & (g == 0))
-            def _():
-                relayed(k, 2, 0).start()
-
-        frame_c[pl.ds(TOP, ROWS), :] = d_one * der[0, g]
-        shifted(frame_c, maps_p)
-        compact(e_two[g] + conv(maps_p, wback[0, g], NN), frame_d, out.at[k, 3, g])
-        leave(k, 3, g)
-        collect(0, g, weight_grad(frame_c[pl.ds(TOP, 256), :], maps_x.at[g]), k == 0)
-
-    def each(function, k, first=0, last=GROUPS, turn=0):
-        def step(i, carry):
-            function(k, (i + turn) % GROUPS if turn else i)
-            return carry
-
-        lax.fori_loop(first, last, step, 0)
+            for _, g in both:
+                exchange(1, 0, g).start()
+
+    def pull_first(k, pair_):
+        both = [(j, 2 * pair_ + j) for j in range(2)]
+        for _, g in both:
+            arrive(k, 2, g)
+        for j, g in both:
+            expand(held.at[k, 2, g], frame_a[j])
+        for j, g in both:
+            d_one = frame_a[j][pl.ds(TOP, ROWS), :] + into[g]
+            compact(d_one, frame_d[j], out.at[k, 2, g])
+            frame_c[j][pl.ds(TOP, ROWS), :] = d_one * der[0, g]
+        for j, _ in both:
+            shifted(frame_c[j], maps_p.at[j])
+        pulled = [conv_back(maps_p.at[j], wback[0, g]) for j, g in both]
+        grads = [weight_grad(frame_c[j][pl.ds(TOP, 256), :], maps_x.at[g]) for j, g in both]
+        for (j, g), value, grad in zip(both, pulled, grads):
+            compact(e_two[g] + value, frame_d[j], out.at[k, 3, g])
+            collect(0, g, grad, k == 0)
+        if k == TICKS - 1:
+            for _, g in both:
+                exchange(0, 0, g).start()
+            for _, g in both:
+                leave(k, 2, g)
+                leave(k, 3, g)
 
     def exchange(which, level, third):
         cut = pl.ds(384 * third, 384)
@@ -346,6 +386,9 @@
                 grad_ref[0, 0, 3 * third + tap] = total[:, tap * W : (tap + 1) * W]
 
     def advance(which, level):
+        if level == 0:
+            for g in range(GROUPS):
+                absorb(which, 0, g)
         for third in range(3):
             if level > 0:
                 absorb(which, level, third)
@@ -353,61 +396,32 @@
                 exchange(which, level + 1, third).start()
 
     pl.semaphore_wait(barrier, 9)
-    xs, ds = (1, 0), (3, 2)
-
-    def rebuild_1(k, g):
-        rebuild(k, g)
-
-        @pl.when(g == 1)
-        def _():
-            pass_on(k - 1, 2, ds)
-
-    each(rebuild, 0)
-    pass_on(0, 1, xs)
-    each(pull_second, 0)
-    pass_on(0, 2, xs)
-    each(pull_first, 0)
-    pass_on(0, 1, ds)
-    each(lambda k, g: leave(k, 2, g), 0, 1)
-    each(rebuild_1, 1)
-    pass_on(1, 1, xs)
-    each(pull_second, 1, turn=1)
-    pass_on(1, 2, xs)
-    each(pull_first, 1)
-    pass_on(1, 1, ds)
-    each(lambda k, g: leave(k, 2, g), 1, 1)
-    last = TICKS - 1
-    each(rebuild_1, last)
-
-    def last_second(k, g):
-        pull_second(k, g)
-        exchange(1, 0, g).start()
-
-        @pl.when(g > 0)
-        def _():
-            absorb(1, 0, g - 1)
-
-    def last_first(k, g):
-        pull_first(k, g)
-        exchange(0, 0, g).start()
-
-        @pl.when(g > 0)
-        def _():
-            absorb(0, 0, g - 1)
-
-    each(last_second, last)
-    absorb(1, 0, 3)
-    advance(1, 0)
-    each(last_first, last, 0, 2)
-    advance(1, 1)
-    each(last_first, last, 2, 4)
-    absorb(0, 0, 3)
-    advance(0, 0)
-    advance(1, 2)
-    advance(0, 1)
-    advance(1, 3)
-    advance(0, 2)
-    advance(0, 3)
+    works = {"R": rebuild, "P2": pull_second, "P1": pull_first}
+
+    def do(token):
+        if token[0] == "S":
+            leave(*token[1:])
+        elif token[0] in ("h1", "h2"):
+            pass_on(*token[1:], int(token[0][1]))
+        else:
+            advance(*token[1:])
+
+    for phase, k, turn, between, after in PLAN:
+
+        def step(i, carry, phase=phase, k=k, turn=turn, between=between):
+            works[phase](k, 1 - i if turn else i)
+            if between:
+
+                @pl.when(i == 0)
+                def _():
+                    for token in between:
+                        do(token)
+
+            return carry
+
+        lax.fori_loop(0, 2, step, 0)
+        for token in after:
+            do(token)
 
     def drain(g, carry):
         for h in range(4):
@@ -418,21 +432,21 @@
 
     @pl.when(section > 0)
     def _():
-        def drain_sent(g, carry):
-            for k in range(TICKS - 1):
-                for h in range(4):
-                    send(k, h, g).wait_send()
-            return carry
-
-        lax.fori_loop(1, GROUPS, drain_sent, 0)
-
-    for hop, condition in enumerate((section > 0, came[0] > 0, came[1] > 0)):
-
-        @pl.when(condition)
+        for k in range(TICKS - 1):
+            for h in range(4):
+                for g in range(GROUPS):
+                    if (h, g) in ROUND[k]:
+                        relayed(k, h, g, 0).wait_send()
+                    else:
+                        send(k, h, g).wait_send()
+
+    for hop in (1, 2):
+
+        @pl.when(came[hop - 1] > 0)
         def _(hop=hop):
             for k in range(TICKS - 1):
-                for h in range(4):
-                    relayed(k, h, hop).wait_send()
+                for h, g in ROUND[k]:
+                    relayed(k, h, g, hop).wait_send()
 
     for which in range(2):
         for level in range(4):
@@ -470,17 +484,17 @@
         scratch_shapes=[
             pltpu.VMEM((2, GROUPS, TAPS, W, W), F32),
             pltpu.VMEM((2, GROUPS, 2 * W, TAPS * W), BF16),
-            pltpu.VMEM((2, GROUPS, TAPS * W, 2 * W), BF16),
+            pltpu.VMEM((2, GROUPS, TAPS * 2 * W, 2 * W), BF16),
             pltpu.VMEM((TICKS, 4, GROUPS, PIX, W), F32),
             pltpu.VMEM((TICKS, 4, GROUPS, PIX, W), F32),
-            pltpu.VMEM((2, TICKS - 1, 4, PIX, W), F32),
+            pltpu.VMEM((2, TICKS - 1, STOPS, PIX, W), F32),
             pltpu.VMEM((GROUPS, 3, 2 * HALF, W), BF16),
             pltpu.VMEM((GROUPS, 3, 2 * HALF, W), BF16),
-            pltpu.VMEM((3, 2 * HALF, W), BF16),
+            pltpu.VMEM((2, 3, 2 * HALF, W), BF16),
             pltpu.VMEM((2, GROUPS, ROWS, W), F32),
             pltpu.VMEM((GROUPS, ROWS, W), F32),
             pltpu.VMEM((GROUPS, ROWS, W), F32),
-            pltpu.VMEM((4, FRAME, W), F32),
+            pltpu.VMEM((4, 2, FRAME, W), F32),
             pltpu.VMEM((2, 2, 2, 2, 2, 32, TAPS * W), F32),
             pltpu.VMEM((2, 2, 2, 2, 32, TAPS * W), F32),
             pltpu.VMEM((2, 3, 2, 2, 32, 384), F32),
@@ -495,8 +509,8 @@
             dma((2, 4, 3)),
             dma((2, GROUPS)),
             dma((2, GROUPS)),
-            dma((3, TICKS - 1, 4)),
-            dma((2, TICKS - 1, 4)),
+            dma((3, TICKS - 1, STOPS)),
+            dma((2, TICKS - 1, STOPS)),
         ],
         compiler_params=pltpu.CompilerParams(
             collective_id=0, has_side_effects=True, vmem_limit_bytes=60 * 2**20

time: 103 us -> 89.4 us (0.87)
  the two profiles are of different devices: /device:TPU:8 before, /device:TPU:25 now
where the time goes in v2:
time: 89.4 us; the launch traced here: 89.3 us
  Pallas kernels  88.6 us (99%)
    pallas_call x1, Pallas kernels, on_device(): pl.pallas_call(kernel, out_shape=(jax.ShapeDtypeStruct(state.shape, F32),...  86.3 us
    pallas_call x1, Pallas kernels, on_device(): pl.pallas_call(hand_out, out_shape=(jax.ShapeDtypeStruct(state.shape, F32...  2.34 us

profile of v2, /device:TPU:25, one launch (start us, length us, event | category | flops | bytes accessed | tf_op | source)
XLA Modules:
  0.0 89.3 jit_solution(14594110774786548356)
XLA Ops:
  0.6 86.3 %relay.1 = (f32[4,196,1,512]{3,2,1,0:T(1,128)}, f32[1,1,9,32,128]{4,3,2,1,0:T(8,128)}, f32[1,1,9,32,128]{4,3,2,1,0:T(8,128)}) custom-call(f32[4,196,1,512]{3,2,1,0:T(1,128)} %bitcast.6, f32[2,4,196,1,512]{4,3,2,1,0:T(1,128)} %bitcast.5, f32[1,1,9,512,128]{4,3,2,1,0:T(8,128)} %first_ref.1, f32[1,1,9,512,128]{4,3,2,1,0:T(8,128)} %second_ref.1), custom_call_target="tpu_custom_call" | custom-call | tf_op jit(solution)/shard_map/relay/pallas_call | solution.py:479
  86.9 2.3 %hand_out.1 = (f32[4,196,1,512]{3,2,1,0:T(1,128)}, f32[1,1,9,32,128]{4,3,2,1,0:T(8,128)}, f32[1,1,9,32,128]{4,3,2,1,0:T(8,128)}) custom-call(f32[4,196,1,512]{3,2,1,0:T(1,128)} %get-tuple-element.9.refs_0_, f32[1,1,9,32,128]{4,3,2,1,0:T(8,128)} %get-tuple-element.10.refs_1_, f32[1,1,9,32,128]{4,3,2,1,0:T(8,128)} %get-tuple-element.11.refs_2_), custom_call_target="tpu_custom_call" | custom-call | tf_op jit(solution)/shard_map/hand_out/pallas_call | solution.py:520

commit v3 on v2

--- a/solution.py
+++ b/solution.py
@@ -17,21 +17,21 @@
 ORDERS = ((0, 1, 2), (1, 2, 0), (2, 0, 1))
 
 ROUND = (
-    ((0, 1), (1, 0), (2, 0)),
-    ((0, 2), (0, 3), (1, 3)),
+    ((1, 0), (1, 2), (2, 1)),
+    ((1, 0), (1, 1), (1, 3)),
 )
 STOPS = 3
 PLAN = (
-    ("R", 0, 0, (), (("h1", 0, 1, 0),)),
-    ("P2", 0, 0, (("h1", 0, 0, 1),), (("h2", 0, 1, 0),)),
-    ("P1", 0, 0, (("S", 0, 3, 0), ("S", 0, 3, 1), ("S", 0, 2, 1), ("h2", 0, 0, 1)), (("S", 0, 2, 0), ("h1", 0, 2, 0), ("S", 0, 3, 3), ("S", 0, 2, 3), ("S", 0, 3, 2))),
-    ("R", 1, 1, (("S", 0, 2, 2), ("h1", 1, 1, 3)), ()),
-    ("P2", 1, 0, (("h1", 1, 0, 2),), (("h1", 1, 0, 3), ("h2", 0, 2, 0))),
-    ("P1", 1, 1, (("S", 1, 3, 3), ("S", 1, 3, 2), ("h2", 1, 0, 2), ("h2", 1, 1, 3)), (("S", 1, 3, 0), ("S", 1, 3, 1), ("h2", 1, 0, 3), ("S", 1, 2, 1))),
-    ("R", 2, 0, (), (("S", 1, 2, 0), ("S", 1, 2, 2), ("S", 1, 2, 3))),
-    ("P2", 2, 0, (), ()),
-    ("P1", 2, 0, (("rs", 1, 0),), (("rs", 0, 0), ("rs", 1, 1), ("rs", 0, 1), ("rs", 1, 2), ("rs", 0, 2), ("rs", 1, 3), ("rs", 0, 3))),
+    ("R", 0, 0, (), ()),
+    ("P2", 0, 0, (("h1", 0, 1, 0),), (("h1", 0, 1, 2),)),
+    ("P1", 0, 0, (), (("h2", 0, 1, 0), ("S", 0, 3, 1), ("S", 0, 3, 3), ("S", 0, 2, 2), ("h2", 0, 1, 2), ("S", 0, 2, 0), ("S", 0, 2, 3), ("S", 0, 3, 0), ("S", 0, 2, 1), ("S", 0, 3, 2))),
+    ("R", 1, 1, (), (("h1", 0, 2, 1), ("h1", 1, 1, 3), ("h2", 0, 2, 1), ("h1", 1, 1, 0), ("h1", 1, 1, 1))),
+    ("P2", 1, 0, (), ()),
+    ("P1", 1, 0, (("S", 1, 3, 1),), (("S", 1, 3, 2), ("S", 1, 3, 0), ("h2", 1, 1, 3), ("h2", 1, 1, 0))),
+    ("R", 2, 1, (("h2", 1, 1, 1), ("S", 1, 3, 3), ("S", 1, 2, 1)), (("S", 1, 2, 2), ("S", 1, 2, 3))),
+    ("P2", 2, 0, (("S", 1, 2, 0),), ()),
 )
+LAST_TURN = 2
 
 
 def split(value):
@@ -94,7 +94,7 @@
 def kernel(
     state_ref, arriving_ref, first_ref, second_ref, ret_ref, fgrad_ref, sgrad_ref,
     raw, wfwd, wback, held, out, stop, maps_y, maps_x, maps_p, der, into, e_two, frames, acc, pair, part1, part2, part3,
-    wsem, lsem, ssem, rsem, osem, xsend, xrecv, psend, precv, hop_send, hop_recv,
+    wsem, lsem, ssem, rsem, osem, xsend, xrecv, psend, precv, lsend, lrecv, hop_send, hop_recv,
 ):
     section, rep = lax.axis_index("section"), lax.axis_index("rep")
     core, z, x = rep % 2, (rep // 2) % 4, rep // 8
@@ -304,7 +304,9 @@
                 exchange(1, 0, g).start()
 
     def pull_first(k, pair_):
-        both = [(j, 2 * pair_ + j) for j in range(2)]
+        pull_first_of(k, [(j, 2 * pair_ + j) for j in range(2)])
+
+    def pull_first_of(k, both):
         for _, g in both:
             arrive(k, 2, g)
         for j, g in both:
@@ -323,7 +325,6 @@
         if k == TICKS - 1:
             for _, g in both:
                 exchange(0, 0, g).start()
-            for _, g in both:
                 leave(k, 2, g)
                 leave(k, 3, g)
 
@@ -343,11 +344,7 @@
         else:
             axis = ORDERS[third][level - 1]
             device = across[axis]
-            if level == 1:
-                index = [slice(None)] * 3
-                index[axis] = 1 - bits[axis]
-                source, target = pair.at[(which, *index, slice(None), cut)], part1.at[which, third]
-            elif level == 2:
+            if level == 2:
                 rest = [a for a in range(3) if a != ORDERS[third][0]]
                 index = [slice(None)] * 2
                 index[rest.index(axis)] = 1 - bits[axis]
@@ -363,8 +360,39 @@
             device_id_type=MESH,
         )
 
+    def spread(which, third, g):
+        place, cut = (g // 2, g % 2), pl.ds(384 * third, 384)
+        if third == 2:
+            source, target = pair.at[which, *place, 1 - bit_a, :, cut], part1.at[which, third, *place]
+        else:
+            source, target = pair.at[which, *place, :, :, cut], part1.at[which, third, place[1 - third]]
+        return pltpu.make_async_remote_copy(
+            src_ref=source,
+            dst_ref=target,
+            send_sem=lsend.at[which, third, g],
+            recv_sem=lrecv.at[which, third, g],
+            device_id=(section, across[third]),
+            device_id_type=MESH,
+        )
+
+    def spreads(which, g, act, mine):
+        for third in range(3):
+            if third == 2:
+                act(spread(which, third, g))
+            else:
+                side = (g // 2, g % 2)[third]
+
+                @pl.when((bits[third] == side) if mine else (bits[third] != side))
+                def _(third=third):
+                    act(spread(which, third, g))
+
+    def cascade(which, g):
+        absorb(which, 0, g)
+        spreads(which, g, lambda copy: copy.start(), False)
+
     def absorb(which, level, third):
-        exchange(which, level, third).wait_recv()
+        if level != 1:
+            exchange(which, level, third).wait_recv()
         cut = pl.ds(384 * third, 384)
         if level == 0:
             pair[which, third // 2, third % 2] += acc[which, core, third // 2, third % 2]
@@ -386,12 +414,11 @@
                 grad_ref[0, 0, 3 * third + tap] = total[:, tap * W : (tap + 1) * W]
 
     def advance(which, level):
-        if level == 0:
+        if level == 1:
             for g in range(GROUPS):
-                absorb(which, 0, g)
+                spreads(which, g, lambda copy: copy.wait_recv(), True)
         for third in range(3):
-            if level > 0:
-                absorb(which, level, third)
+            absorb(which, level, third)
             if level < 3:
                 exchange(which, level + 1, third).start()
 
@@ -401,10 +428,8 @@
     def do(token):
         if token[0] == "S":
             leave(*token[1:])
-        elif token[0] in ("h1", "h2"):
+        else:
             pass_on(*token[1:], int(token[0][1]))
-        else:
-            advance(*token[1:])
 
     for phase, k, turn, between, after in PLAN:
 
@@ -422,6 +447,31 @@
         lax.fori_loop(0, 2, step, 0)
         for token in after:
             do(token)
+
+    for g in range(GROUPS):
+        cascade(1, g)
+
+    def finish(i, carry):
+        g = (i + LAST_TURN) % GROUPS
+        pull_first_of(TICKS - 1, [(0, g)])
+
+        @pl.when(i > 0)
+        def _():
+            cascade(0, (i + LAST_TURN + GROUPS - 1) % GROUPS)
+
+        @pl.when(i == 2)
+        def _():
+            advance(1, 1)
+
+        return carry
+
+    lax.fori_loop(0, GROUPS, finish, 0)
+    cascade(0, (GROUPS - 1 + LAST_TURN) % GROUPS)
+    advance(1, 2)
+    advance(0, 1)
+    advance(1, 3)
+    advance(0, 2)
+    advance(0, 3)
 
     def drain(g, carry):
         for h in range(4):
@@ -449,8 +499,11 @@
                     relayed(k, h, g, hop).wait_send()
 
     for which in range(2):
-        for level in range(4):
-            for third in range(3 if level else GROUPS):
+        for g in range(GROUPS):
+            exchange(which, 0, g).wait_send()
+            spreads(which, g, lambda copy: copy.wait_send(), False)
+        for level in (2, 3):
+            for third in range(3):
                 exchange(which, level, third).wait_send()
 
 
@@ -509,6 +562,8 @@
             dma((2, 4, 3)),
             dma((2, GROUPS)),
             dma((2, GROUPS)),
+            dma((2, 3, GROUPS)),
+            dma((2, 3, GROUPS)),
             dma((3, TICKS - 1, STOPS)),
             dma((2, TICKS - 1, STOPS)),
         ],

time: 89.4 us -> 90.3 us (1.010)
  the two profiles are of different devices: /device:TPU:25 before, /device:TPU:6 now
where the time goes in v3:
time: 90.3 us; the launch traced here: 90.2 us
  Pallas kernels  89.5 us (99%)
    pallas_call x1, Pallas kernels, on_device(): pl.pallas_call(kernel, out_shape=(jax.ShapeDtypeStruct(state.shape, F32),...  87.2 us
    pallas_call x1, Pallas kernels, on_device(): pl.pallas_call(hand_out, out_shape=(jax.ShapeDtypeStruct(state.shape, F32...  2.34 us

profile of v3, /device:TPU:6, one launch (start us, length us, event | category | flops | bytes accessed | tf_op | source)
XLA Modules:
  0.0 90.2 jit_solution(1422227592043179143)
XLA Ops:
  0.6 87.2 %relay.1 = (f32[4,196,1,512]{3,2,1,0:T(1,128)}, f32[1,1,9,32,128]{4,3,2,1,0:T(8,128)}, f32[1,1,9,32,128]{4,3,2,1,0:T(8,128)}) custom-call(f32[4,196,1,512]{3,2,1,0:T(1,128)} %bitcast.6, f32[2,4,196,1,512]{4,3,2,1,0:T(1,128)} %bitcast.5, f32[1,1,9,512,128]{4,3,2,1,0:T(8,128)} %first_ref.1, f32[1,1,9,512,128]{4,3,2,1,0:T(8,128)} %second_ref.1), custom_call_target="tpu_custom_call" | custom-call | tf_op jit(solution)/shard_map/relay/pallas_call | solution.py:532
  87.8 2.3 %hand_out.1 = (f32[4,196,1,512]{3,2,1,0:T(1,128)}, f32[1,1,9,32,128]{4,3,2,1,0:T(8,128)}, f32[1,1,9,32,128]{4,3,2,1,0:T(8,128)}) custom-call(f32[4,196,1,512]{3,2,1,0:T(1,128)} %get-tuple-element.9.refs_0_, f32[1,1,9,32,128]{4,3,2,1,0:T(8,128)} %get-tuple-element.10.refs_1_, f32[1,1,9,32,128]{4,3,2,1,0:T(8,128)} %get-tuple-element.11.refs_2_), custom_call_target="tpu_custom_call" | custom-call | tf_op jit(solution)/shard_map/hand_out/pallas_call | solution.py:575

commit v4 on v3

--- a/solution.py
+++ b/solution.py
@@ -15,23 +15,61 @@
 FRAME = 304
 HALF = 288
 ORDERS = ((0, 1, 2), (1, 2, 0), (2, 0, 1))
+PARTS = ((0, 2), (2, 3), (5, 4))
 
 ROUND = (
-    ((1, 0), (1, 2), (2, 1)),
-    ((1, 0), (1, 1), (1, 3)),
+    ((0, 0), (1, 2), (2, 0)),
+    ((0, 2), (1, 2), (1, 3)),
 )
 STOPS = 3
 PLAN = (
-    ("R", 0, 0, (), ()),
-    ("P2", 0, 0, (("h1", 0, 1, 0),), (("h1", 0, 1, 2),)),
-    ("P1", 0, 0, (), (("h2", 0, 1, 0), ("S", 0, 3, 1), ("S", 0, 3, 3), ("S", 0, 2, 2), ("h2", 0, 1, 2), ("S", 0, 2, 0), ("S", 0, 2, 3), ("S", 0, 3, 0), ("S", 0, 2, 1), ("S", 0, 3, 2))),
-    ("R", 1, 1, (), (("h1", 0, 2, 1), ("h1", 1, 1, 3), ("h2", 0, 2, 1), ("h1", 1, 1, 0), ("h1", 1, 1, 1))),
-    ("P2", 1, 0, (), ()),
-    ("P1", 1, 0, (("S", 1, 3, 1),), (("S", 1, 3, 2), ("S", 1, 3, 0), ("h2", 1, 1, 3), ("h2", 1, 1, 0))),
-    ("R", 2, 1, (("h2", 1, 1, 1), ("S", 1, 3, 3), ("S", 1, 2, 1)), (("S", 1, 2, 2), ("S", 1, 2, 3))),
-    ("P2", 2, 0, (("S", 1, 2, 0),), ()),
+    ("R", 0, 1),
+    ("R", 0, 0),
+    ("h1", 0, 1, 2),
+    ("P2", 0, 1),
+    ("P1", 0, 1),
+    ("h1", 0, 0, 0),
+    ("P2", 0, 0),
+    ("S", 0, 2, 2),
+    ("S", 0, 3, 2),
+    ("h2", 0, 1, 2),
+    ("S", 0, 3, 3),
+    ("P1", 0, 0),
+    ("S", 0, 3, 0),
+    ("h2", 0, 0, 0),
+    ("S", 0, 3, 1),
+    ("S", 0, 2, 0),
+    ("S", 0, 2, 3),
+    ("R", 1, 1),
+    ("S", 0, 2, 1),
+    ("h1", 0, 2, 0),
+    ("h1", 1, 1, 3),
+    ("P2", 1, 1),
+    ("R", 1, 0),
+    ("h2", 0, 2, 0),
+    ("h1", 1, 1, 2),
+    ("P2", 1, 0),
+    ("P1", 1, 1),
+    ("S", 1, 3, 3),
+    ("h1", 1, 0, 2),
+    ("P1", 1, 0),
+    ("S", 1, 3, 2),
+    ("h2", 1, 1, 2),
+    ("S", 1, 3, 1),
+    ("S", 1, 3, 0),
+    ("h2", 1, 0, 2),
+    ("S", 1, 2, 0),
+    ("h2", 1, 1, 3),
+    ("R", 2, 0),
+    ("R", 2, 1),
+    ("S", 1, 2, 1),
+    ("S", 1, 2, 2),
+    ("S", 1, 2, 3),
+    ("P2", 2, 1),
+    ("P2", 2, 0),
+    ("P1", 2, 0),
+    ("P1", 2, 1),
 )
-LAST_TURN = 2
 
 
 def split(value):
@@ -218,17 +256,11 @@
             save(h, g).start()
             return
 
-        direct = section > 0
-        for group in [g_ for h_, g_ in ROUND[k] if h_ == h]:
-            direct = direct & (g != group)
-
-            @pl.when((section > 0) & (g == group))
-            def _(group=group):
-                relayed(k, h, group, 0).start()
-
-        @pl.when(direct)
+        copy = relayed(k, h, g, 0) if (h, g) in ROUND[k] else send(k, h, g)
+
+        @pl.when(section > 0)
         def _():
-            send(k, h, g).start()
+            copy.start()
 
     def prepare(which, g):
         load_weight(which, g).wait()
@@ -254,7 +286,14 @@
             place[...] = rows if fresh else place[...] + rows
 
     def rebuild(k, pair_):
-        both = [(j, 2 * pair_ + j) for j in range(2)]
+        groups = [(j, 2 * pair_ + j) for j in range(2)]
+        if (k, pair_) == PLAN[0][1:]:
+            rebuild_of(k, groups[:1], True)
+            rebuild_of(k, groups[1:], False)
+        else:
+            rebuild_of(k, groups, False)
+
+    def rebuild_of(k, both, first):
         for _, g in both:
             arrive(k, 1, g)
             arrive(k, 0, g)
@@ -269,9 +308,12 @@
         for (j, g), (act, slope) in zip(both, acts):
             der[1, g] = slope
             compact(jnp.where(inside, frame_b[j][pl.ds(TOP, ROWS), :] - act, 0.0), frame_c[j], out.at[k, 1, g])
+        if first:
+            pl.semaphore_wait(barrier, 9)
         for _, g in both:
             leave(k, 1, g)
-            if k == 0:
+        if k == 0:
+            for _, g in both:
                 prepare(0, g)
         for j, g in both:
             shifted(frame_c[j], maps_x.at[g])
@@ -317,19 +359,25 @@
             frame_c[j][pl.ds(TOP, ROWS), :] = d_one * der[0, g]
         for j, _ in both:
             shifted(frame_c[j], maps_p.at[j])
-        pulled = [conv_back(maps_p.at[j], wback[0, g]) for j, g in both]
-        grads = [weight_grad(frame_c[j][pl.ds(TOP, 256), :], maps_x.at[g]) for j, g in both]
-        for (j, g), value, grad in zip(both, pulled, grads):
-            compact(e_two[g] + value, frame_d[j], out.at[k, 3, g])
-            collect(0, g, grad, k == 0)
-        if k == TICKS - 1:
-            for _, g in both:
+        last = k == TICKS - 1
+        if last:
+            for j, g in both:
+                collect(0, g, weight_grad(frame_c[j][pl.ds(TOP, 256), :], maps_x.at[g]), False)
                 exchange(0, 0, g).start()
                 leave(k, 2, g)
+        pulled = [conv_back(maps_p.at[j], wback[0, g]) for j, g in both]
+        if not last:
+            grads = [weight_grad(frame_c[j][pl.ds(TOP, 256), :], maps_x.at[g]) for j, g in both]
+        for j, g in both:
+            compact(e_two[g] + pulled[j], frame_d[j], out.at[k, 3, g])
+            if last:
                 leave(k, 3, g)
+            else:
+                collect(0, g, grads[j], k == 0)
 
     def exchange(which, level, third):
-        cut = pl.ds(384 * third, 384)
+        first, count = PARTS[third % 3] if level else (0, TAPS)
+        cut, width = pl.ds(W * first, W * count), pl.ds(0, W * count)
         if level == 0:
             g = third
             source, target = acc.at[which, 1 - core, g // 2, g % 2], pair.at[which, g // 2, g % 2]
@@ -348,9 +396,11 @@
                 rest = [a for a in range(3) if a != ORDERS[third][0]]
                 index = [slice(None)] * 2
                 index[rest.index(axis)] = 1 - bits[axis]
-                source, target = part1.at[(which, third, *index)], part2.at[which, third]
+                source = part1.at[(which, third, *index, slice(None), width)]
+                target = part2.at[which, third, :, :, width]
             else:
-                source, target = part2.at[which, third, 1 - bits[axis]], part3.at[which, third]
+                source = part2.at[which, third, 1 - bits[axis], :, width]
+                target = part3.at[which, third, :, width]
         return pltpu.make_async_remote_copy(
             src_ref=source,
             dst_ref=target,
@@ -361,11 +411,14 @@
         )
 
     def spread(which, third, g):
-        place, cut = (g // 2, g % 2), pl.ds(384 * third, 384)
+        place, (first, count) = (g // 2, g % 2), PARTS[third]
+        cut, width = pl.ds(W * first, W * count), pl.ds(0, W * count)
         if third == 2:
-            source, target = pair.at[which, *place, 1 - bit_a, :, cut], part1.at[which, third, *place]
+            source = pair.at[which, *place, 1 - bit_a, :, cut]
+            target = part1.at[which, third, *place, :, width]
         else:
-            source, target = pair.at[which, *place, :, :, cut], part1.at[which, third, place[1 - third]]
+            source = pair.at[which, *place, :, :, cut]
+            target = part1.at[which, third, place[1 - third], :, :, width]
         return pltpu.make_async_remote_copy(
             src_ref=source,
             dst_ref=target,
@@ -375,8 +428,8 @@
             device_id_type=MESH,
         )
 
-    def spreads(which, g, act, mine):
-        for third in range(3):
+    def spreads(which, g, act, mine, thirds=range(3)):
+        for third in thirds:
             if third == 2:
                 act(spread(which, third, g))
             else:
@@ -391,82 +444,67 @@
         spreads(which, g, lambda copy: copy.start(), False)
 
     def absorb(which, level, third):
-        if level != 1:
+        if level == 1:
+            for g in range(GROUPS):
+                spreads(which, g, lambda copy: copy.wait_recv(), True, (third,))
+        else:
             exchange(which, level, third).wait_recv()
-        cut = pl.ds(384 * third, 384)
         if level == 0:
             pair[which, third // 2, third % 2] += acc[which, core, third // 2, third % 2]
             return
+        first, count = PARTS[third]
+        cut, width = pl.ds(W * first, W * count), pl.ds(0, W * count)
         axis = ORDERS[third][level - 1]
         if level == 1:
             index = [slice(None)] * 3
             index[axis] = bits[axis]
-            part1[which, third] += pair[(which, *index, slice(None), cut)]
+            part1[which, third, :, :, :, width] += pair[(which, *index, slice(None), cut)]
         elif level == 2:
             rest = [a for a in range(3) if a != ORDERS[third][0]]
             index = [slice(None)] * 2
             index[rest.index(axis)] = bits[axis]
-            part2[which, third] += part1[(which, third, *index)]
+            part2[which, third, :, :, width] += part1[(which, third, *index, slice(None), width)]
         else:
-            total = part3[which, third] + part2[which, third, bits[axis]]
+            total = part3[which, third, :, width] + part2[which, third, bits[axis], :, width]
             grad_ref = (fgrad_ref, sgrad_ref)[which]
-            for tap in range(3):
-                grad_ref[0, 0, 3 * third + tap] = total[:, tap * W : (tap + 1) * W]
+            for tap in range(count):
+                grad_ref[0, 0, first + tap] = total[:, tap * W : (tap + 1) * W]
 
     def advance(which, level):
-        if level == 1:
-            for g in range(GROUPS):
-                spreads(which, g, lambda copy: copy.wait_recv(), True)
-        for third in range(3):
+        for third in (2, 1, 0):
             absorb(which, level, third)
             if level < 3:
                 exchange(which, level + 1, third).start()
 
-    pl.semaphore_wait(barrier, 9)
     works = {"R": rebuild, "P2": pull_second, "P1": pull_first}
 
-    def do(token):
-        if token[0] == "S":
+    order = [2 * token[2] + j for token in PLAN if token[:2] == ("P1", TICKS - 1) for j in range(2)]
+    reduced = []
+    for token in PLAN:
+        kind = token[0]
+        if kind == "S":
             leave(*token[1:])
-        else:
-            pass_on(*token[1:], int(token[0][1]))
-
-    for phase, k, turn, between, after in PLAN:
-
-        def step(i, carry, phase=phase, k=k, turn=turn, between=between):
-            works[phase](k, 1 - i if turn else i)
-            if between:
-
-                @pl.when(i == 0)
-                def _():
-                    for token in between:
-                        do(token)
-
-            return carry
-
-        lax.fori_loop(0, 2, step, 0)
-        for token in after:
-            do(token)
-
-    for g in range(GROUPS):
-        cascade(1, g)
-
-    def finish(i, carry):
-        g = (i + LAST_TURN) % GROUPS
-        pull_first_of(TICKS - 1, [(0, g)])
-
-        @pl.when(i > 0)
-        def _():
-            cascade(0, (i + LAST_TURN + GROUPS - 1) % GROUPS)
-
-        @pl.when(i == 2)
-        def _():
-            advance(1, 1)
-
-        return carry
-
-    lax.fori_loop(0, GROUPS, finish, 0)
-    cascade(0, (GROUPS - 1 + LAST_TURN) % GROUPS)
+            continue
+        if kind in ("h1", "h2"):
+            pass_on(*token[1:], int(kind[1]))
+            continue
+        for g in reduced:
+            cascade(1, g)
+        reduced = []
+        k, pair_ = token[1:]
+        if k < TICKS - 1 or kind != "P1":
+            works[kind](k, pair_)
+            if k == TICKS - 1 and kind == "P2":
+                reduced = [2 * pair_, 2 * pair_ + 1]
+            continue
+        for g in (2 * pair_, 2 * pair_ + 1):
+            i = order.index(g)
+            pull_first_of(k, [(0, g)])
+            if i:
+                cascade(0, order[i - 1])
+            if i == 2:
+                advance(1, 1)
+    cascade(0, order[-1])
     advance(1, 2)
     advance(0, 1)
     advance(1, 3)
@@ -550,9 +588,9 @@
             pltpu.VMEM((4, 2, FRAME, W), F32),
             pltpu.VMEM((2, 2, 2, 2, 2, 32, TAPS * W), F32),
             pltpu.VMEM((2, 2, 2, 2, 32, TAPS * W), F32),
-            pltpu.VMEM((2, 3, 2, 2, 32, 384), F32),
-            pltpu.VMEM((2, 3, 2, 32, 384), F32),
-            pltpu.VMEM((2, 3, 32, 384), F32),
+            pltpu.VMEM((2, 3, 2, 2, 32, 4 * W), F32),
+            pltpu.VMEM((2, 3, 2, 32, 4 * W), F32),
+            pltpu.VMEM((2, 3, 32, 4 * W), F32),
             dma((2, GROUPS)),
             dma((4, GROUPS)),
             dma((TICKS - 1, 4, GROUPS)),

time: 90.3 us -> 89 us (0.986)
  Pallas kernels: 89.5 us -> 88.1 us
    pallas_call x1, Pallas kernels: 87.2 us -> 85.8 us  [on_device(): pl.pallas_call(kernel, out_shape=(jax.ShapeDtypeStruct(state.shape, F32),...]
where the time goes in v4:
time: 89 us; the launch traced here: 88.9 us
  Pallas kernels  88.1 us (99%)
    pallas_call x1, Pallas kernels, on_device(): pl.pallas_call(kernel, out_shape=(jax.ShapeDtypeStruct(state.shape, F32),...  85.8 us
    pallas_call x1, Pallas kernels, on_device(): pl.pallas_call(hand_out, out_shape=(jax.ShapeDtypeStruct(state.shape, F32...  2.34 us

profile of v4, /device:TPU:6, one launch (start us, length us, event | category | flops | bytes accessed | tf_op | source)
XLA Modules:
  0.0 88.9 jit_solution(9740981248102444121)
XLA Ops:
  0.6 85.8 %relay.1 = (f32[4,196,1,512]{3,2,1,0:T(1,128)}, f32[1,1,9,32,128]{4,3,2,1,0:T(8,128)}, f32[1,1,9,32,128]{4,3,2,1,0:T(8,128)}) custom-call(f32[4,196,1,512]{3,2,1,0:T(1,128)} %bitcast.6, f32[2,4,196,1,512]{4,3,2,1,0:T(1,128)} %bitcast.5, f32[1,1,9,512,128]{4,3,2,1,0:T(8,128)} %first_ref.1, f32[1,1,9,512,128]{4,3,2,1,0:T(8,128)} %second_ref.1), custom_call_target="tpu_custom_call" | custom-call | tf_op jit(solution)/shard_map/relay/pallas_call | solution.py:570
  86.4 2.3 %hand_out.1 = (f32[4,196,1,512]{3,2,1,0:T(1,128)}, f32[1,1,9,32,128]{4,3,2,1,0:T(8,128)}, f32[1,1,9,32,128]{4,3,2,1,0:T(8,128)}) custom-call(f32[4,196,1,512]{3,2,1,0:T(1,128)} %get-tuple-element.9.refs_0_, f32[1,1,9,32,128]{4,3,2,1,0:T(8,128)} %get-tuple-element.10.refs_1_, f32[1,1,9,32,128]{4,3,2,1,0:T(8,128)} %get-tuple-element.11.refs_2_), custom_call_target="tpu_custom_call" | custom-call | tf_op jit(solution)/shard_map/hand_out/pallas_call | solution.py:613

commit v5 on v4

--- a/solution.py
+++ b/solution.py
@@ -15,7 +15,7 @@
 FRAME = 304
 HALF = 288
 ORDERS = ((0, 1, 2), (1, 2, 0), (2, 0, 1))
-PARTS = ((0, 2), (2, 3), (5, 4))
+PARTS = ((0, 3), (3, 3), (6, 3))
 
 ROUND = (
     ((0, 0), (1, 2), (2, 0)),
@@ -213,12 +213,13 @@
     def save(h, g):
         return pltpu.make_async_copy(out.at[2, h, g], ret_ref.at[h, :, 0, lanes(g)], osem.at[h, g])
 
-    for g in range(GROUPS):
-        load_state(0, g).start()
+    sooner = [(g + 2 * PLAN[0][2]) % GROUPS for g in range(GROUPS)]
+    for g in sooner:
         load_weight(1, g).start()
         load_state(1, g).start()
+        load_state(0, g).start()
         load_weight(0, g).start()
-    for g in range(GROUPS):
+    for g in sooner:
         load_state(3, g).start()
         load_state(2, g).start()
 
@@ -588,9 +589,9 @@
             pltpu.VMEM((4, 2, FRAME, W), F32),
             pltpu.VMEM((2, 2, 2, 2, 2, 32, TAPS * W), F32),
             pltpu.VMEM((2, 2, 2, 2, 32, TAPS * W), F32),
-            pltpu.VMEM((2, 3, 2, 2, 32, 4 * W), F32),
-            pltpu.VMEM((2, 3, 2, 32, 4 * W), F32),
-            pltpu.VMEM((2, 3, 32, 4 * W), F32),
+            pltpu.VMEM((2, 3, 2, 2, 32, 3 * W), F32),
+            pltpu.VMEM((2, 3, 2, 32, 3 * W), F32),
+            pltpu.VMEM((2, 3, 32, 3 * W), F32),
             dma((2, GROUPS)),
             dma((4, GROUPS)),
             dma((TICKS - 1, 4, GROUPS)),

time: 89 us -> 91.2 us (1.025)
  Pallas kernels: 88.1 us -> 89.7 us
    pallas_call x1, Pallas kernels: 85.8 us -> 87.3 us  [on_device(): pl.pallas_call(kernel, out_shape=(jax.ShapeDtypeStruct(state.shape, F32),...]
where the time goes in v5:
time: 91.2 us; the launch traced here: 90.5 us
  Pallas kernels  89.7 us (98%)
    pallas_call x1, Pallas kernels, on_device(): pl.pallas_call(kernel, out_shape=(jax.ShapeDtypeStruct(state.shape, F32),...  87.3 us
    pallas_call x1, Pallas kernels, on_device(): pl.pallas_call(hand_out, out_shape=(jax.ShapeDtypeStruct(state.shape, F32...  2.34 us

profile of v5, /device:TPU:6, one launch (start us, length us, event | category | flops | bytes accessed | tf_op | source)
XLA Modules:
  0.0 90.5 jit_solution(7946385012436744678)
XLA Ops:
  0.6 87.3 %relay.1 = (f32[4,196,1,512]{3,2,1,0:T(1,128)}, f32[1,1,9,32,128]{4,3,2,1,0:T(8,128)}, f32[1,1,9,32,128]{4,3,2,1,0:T(8,128)}) custom-call(f32[4,196,1,512]{3,2,1,0:T(1,128)} %bitcast.6, f32[2,4,196,1,512]{4,3,2,1,0:T(1,128)} %bitcast.5, f32[1,1,9,512,128]{4,3,2,1,0:T(8,128)} %first_ref.1, f32[1,1,9,512,128]{4,3,2,1,0:T(8,128)} %second_ref.1), custom_call_target="tpu_custom_call" | custom-call | tf_op jit(solution)/shard_map/relay/pallas_call | solution.py:571
  88.0 2.3 %hand_out.1 = (f32[4,196,1,512]{3,2,1,0:T(1,128)}, f32[1,1,9,32,128]{4,3,2,1,0:T(8,128)}, f32[1,1,9,32,128]{4,3,2,1,0:T(8,128)}) custom-call(f32[4,196,1,512]{3,2,1,0:T(1,128)} %get-tuple-element.9.refs_0_, f32[1,1,9,32,128]{4,3,2,1,0:T(8,128)} %get-tuple-element.10.refs_1_, f32[1,1,9,32,128]{4,3,2,1,0:T(8,128)} %get-tuple-element.11.refs_2_), custom_call_target="tpu_custom_call" | custom-call | tf_op jit(solution)/shard_map/hand_out/pallas_call | solution.py:614
